TPU v7x, 32 devices: a whole 2x2x4 slice. The times are simulated.
32 devices in a mesh: shot: 2 (over y), gx: 4 (over z), gy: 4 (over x, core).
Axes of the slice: x: 2, y: 2, z: 4, core: 2. Of those that a mesh axis runs over, the one named last changes fastest.
Arguments:
- source_prev: float32 [64, 32, 320], P(('shot', 'gx'), 'gy'), parts along dimension 0, may hold values from -0.6 to 0.6
- source_now: float32 [64, 32, 320], P(('shot', 'gx'), 'gy'), parts along dimension 0, may hold values from -0.6 to 0.6
- receiver_prev: float32 [64, 32, 320], P(('shot', 'gx'), 'gy'), parts along dimension 0, may hold values from -6 to 6
- receiver_now: float32 [64, 32, 320], P(('shot', 'gx'), 'gy'), parts along dimension 0, may hold values from -6 to 6
- speed_squared: float32 [64, 32, 320], P(('shot', 'gx'), 'gy'), parts along dimension 0, may hold values from 0.05 to 0.18
- wavelet: float32 [20], P('shot'), parts along dimension 0, may hold values from -40 to 40
- source_cell: int32 [2], P('shot'), parts along dimension 0, may hold values from 0 to 327679
- traces: float32 [20, 1024], P('shot', ('gx', 'gy')), parts along dimension 0, may hold values from -18 to 18
- receiver_cells: int32 [2, 1024], P('shot', ('gx', 'gy')), parts along dimension 0, may hold values from 0 to 1023
- plan: int32 [8], P('shot'), parts along dimension 0, may hold values from 0 to 9, as said below
- stored_snapshots: bfloat16 [8, 32, 32, 320], P('shot', 'gx', 'gy'), parts along dimension 0, may hold values from -6 to 6
- image_before: float32 [64, 32, 320], P(('shot', 'gx'), 'gy'), parts along dimension 0, may hold values from -6 to 6
Outputs:
- new_source_prev: float32 [64, 32, 320], P(('shot', 'gx'), 'gy'), parts along dimension 0
- new_source_now: float32 [64, 32, 320], P(('shot', 'gx'), 'gy'), parts along dimension 0
- new_receiver_prev: float32 [64, 32, 320], P(('shot', 'gx'), 'gy'), parts along dimension 0
- new_receiver_now: float32 [64, 32, 320], P(('shot', 'gx'), 'gy'), parts along dimension 0
- snapshots: bfloat16 [8, 32, 32, 320], P('shot', 'gx', 'gy'), parts along dimension 0
- image: float32 [64, 32, 320], P(('shot', 'gx'), 'gy'), parts along dimension 0
There are 2 independent parts, one for each index of `shot`. A program takes and returns all parts, laid end to end along the dimension named above; each array names one. Nothing has to cross between parts.
Inputs may be any that keep to these rules, and one draw needn't show every extreme that they name: `plan`: 4 different steps in increasing order; the first is 0 and the last is 9.
All inputs are finite; a program needn't handle non-finite values.
Results may differ from a plain program's by a relative error of at most 0.001.
Values sent between devices are 32-bit elements; how exact they have to be, the bound alone decides.
A program may use at most 64 MiB of HBM per device.

v0:
```python
import functools
import jax
import jax.numpy as jnp
from jax import lax
from jax.experimental import pallas as pl
from jax.experimental.pallas import tpu as pltpu
from jax.sharding import PartitionSpec as P

STENCIL_COEFFS = (-205.0 / 72.0, 8.0 / 5.0, -1.0 / 5.0, 8.0 / 315.0, -1.0 / 560.0)
LANES = 128
HALF = 4
LOW_X, HIGH_X, LOW_Y, HIGH_Y = range(4)
OPPOSITE = (HIGH_X, LOW_X, HIGH_Y, LOW_Y)
MESH = pl.DeviceIdType.MESH


def kernel(
    total_steps,
    source_prev_hbm,
    source_now_hbm,
    receiver_prev_hbm,
    receiver_now_hbm,
    speed_hbm,
    wavelet_hbm,
    source_cell,
    traces_hbm,
    receiver_cells_hbm,
    hist,
    speed,
    core,
    sides,
    packed,
    landed,
    records,
    gathered,
    planes,
    inject,
    send_sem,
    recv_sem,
    trace_send,
    trace_recv,
    load_sem,
    source_prev,
    source_now,
    receiver_prev,
    receiver_now,
    speed_squared,
    wavelet,
    traces,
    receiver_cells,
):
    loads = [
        pltpu.make_async_copy(start, end, load_sem.at[i])
        for i, (start, end) in enumerate(
            (
                (source_now_hbm, source_now),
                (receiver_now_hbm, receiver_now),
                (traces_hbm, traces),
                (receiver_cells_hbm, receiver_cells),
                (source_prev_hbm, source_prev),
                (receiver_prev_hbm, receiver_prev),
                (speed_hbm, speed_squared),
                (wavelet_hbm, wavelet),
            )
        )
    ]
    for load in loads:
        load.start()
    block_x, block_y, depth = source_now.shape
    count_x, count_y = lax.axis_size("gx"), lax.axis_size("gy")
    me_x, me_y = lax.axis_index("gx"), lax.axis_index("gy")
    grid_y = block_y * count_y
    peers = count_x * count_y
    me = me_x * count_y + me_y
    width = speed.shape[2]
    full = depth // LANES
    own = traces.shape[1]
    exists = (me_x > 0, me_x < count_x - 1, me_y > 0, me_y < count_y - 1)
    there = ({"gx": me_x - 1}, {"gx": me_x + 1}, {"gy": me_y - 1}, {"gy": me_y + 1})

    def peer_of(offset):
        other = lax.rem(me + offset, peers)
        return {"gx": other // count_y, "gy": lax.rem(other, count_y)}

    barrier = pltpu.get_barrier_semaphore()

    def greet(offset, carry):
        pl.semaphore_signal(barrier, inc=1, device_id=peer_of(offset), device_id_type=MESH)
        return carry

    for side in range(4):

        @pl.when(jnp.logical_not(exists[side]))
        def _():
            for field in range(2):
                for parity in range(2):
                    landed[field, parity, side] = jnp.zeros(landed.shape[3:], jnp.float32)

    lax.fori_loop(1, peers, greet, 0)

    row = lax.broadcasted_iota(jnp.int32, (block_y, width), 0)
    lane = lax.broadcasted_iota(jnp.int32, (block_y, width), 1)
    first_half = row < HALF
    tail_lane = lax.broadcasted_iota(jnp.int32, (block_y, LANES), 1)
    in_tail = tail_lane < LANES // 2

    def place(field, index, array):
        hist[field, index, HALF : HALF + block_x, :, full * LANES :] = jnp.zeros(
            (block_x, block_y, width - full * LANES), jnp.float32
        )
        hist[field, index, HALF : HALF + block_x, :, 0:depth] = array[...]

    for load in loads[:4]:
        load.wait()
    place(0, 1, source_now)
    place(1, 1, receiver_now)
    records[...] = jnp.zeros_like(records)
    records[0:total_steps, :] = traces[...]
    records[total_steps : total_steps + 1, :] = receiver_cells[...].astype(jnp.float32)
    def halo_copy(field, parity, side):
        return pltpu.make_async_remote_copy(
            src_ref=packed.at[field, side],
            dst_ref=landed.at[field, parity, OPPOSITE[side]],
            send_sem=send_sem.at[field, side],
            recv_sem=recv_sem.at[field, parity, OPPOSITE[side]],
            device_id=there[side],
            device_id_type=MESH,
        )

    def arrival(field, parity, side):
        return pltpu.make_async_remote_copy(
            src_ref=packed.at[field, side],
            dst_ref=landed.at[field, parity, side],
            send_sem=send_sem.at[field, side],
            recv_sem=recv_sem.at[field, parity, side],
            device_id=there[side],
            device_id_type=MESH,
        )

    def pack(field, side, tiles):
        for i in range(HALF):
            for j in range(full):
                packed[field, side, i * full + j] = tiles[i][:, j * LANES : (j + 1) * LANES]
        tails = [tile[:, full * LANES :] for tile in tiles]
        for i in range(2):
            packed[field, side, HALF * full + i] = tails[i] + pltpu.roll(
                tails[i + 2], LANES // 2, axis=1
            )

    def unpack(field, parity, side):
        tails = []
        for i in range(2):
            both = landed[field, parity, side, HALF * full + i]
            tails.append((both, pltpu.roll(both, LANES // 2, axis=1)))
        result = []
        for i in range(HALF):
            tail = jnp.where(in_tail, tails[i % 2][i // 2], 0.0)
            result.append(
                jnp.concatenate(
                    [landed[field, parity, side, i * full + j] for j in range(full)] + [tail],
                    axis=1,
                )
            )
        return result

    def send(field, index, parity):
        tiles = [hist[field, index, HALF + x] for x in range(block_x)]
        pack(field, LOW_X, tiles[:HALF])
        pack(field, HIGH_X, tiles[block_x - HALF :])
        turned = [pltpu.roll(tiles[i + HALF], HALF, axis=0) for i in range(HALF)]
        pack(field, LOW_Y, [jnp.where(first_half, tiles[i], turned[i]) for i in range(HALF)])
        pack(field, HIGH_Y, [jnp.where(first_half, turned[i], tiles[i]) for i in range(HALF)])
        for side in range(4):

            @pl.when(exists[side])
            def _():
                halo_copy(field, parity, side).start()

    def receive(field, index, parity):
        for side in range(4):

            @pl.when(exists[side])
            def _():
                arrival(field, parity, side).wait()

        low, high = unpack(field, parity, LOW_X), unpack(field, parity, HIGH_X)
        for i in range(HALF):
            hist[field, index, i] = low[i]
            hist[field, index, HALF + block_x + i] = high[i]
        low, high = unpack(field, parity, LOW_Y), unpack(field, parity, HIGH_Y)
        for i in range(HALF):
            sides[field, i] = jnp.where(first_half, high[i], low[i])
            sides[field, i + HALF] = pltpu.roll(
                jnp.where(first_half, low[i], high[i]), HALF, axis=0
            )

    def advance(field, index, extra):
        for x in range(block_x):
            center = hist[field, index, HALF + x]
            side = sides[field, x]
            spread = 3.0 * STENCIL_COEFFS[0] * center
            for k in range(1, HALF + 1):
                around = hist[field, index, HALF + x - k] + hist[field, index, HALF + x + k]
                around += pltpu.roll(center, k, axis=1) + pltpu.roll(center, width - k, axis=1)
                around += pltpu.roll(jnp.where(row < block_y - k, center, side), k, axis=0)
                around += pltpu.roll(jnp.where(row < k, side, center), block_y - k, axis=0)
                spread += STENCIL_COEFFS[k] * around
            latest = 2.0 * center - hist[field, index - 1, HALF + x] + speed[x] * spread
            hist[field, index + 1, HALF + x] = extra(x, latest)

    pl.semaphore_wait(barrier, peers - 1)
    send(0, 1, 0)
    send(1, 1, 0)

    def trace_copy(offset):
        return pltpu.make_async_remote_copy(
            src_ref=records,
            dst_ref=gathered.at[offset - 1],
            send_sem=trace_send,
            recv_sem=trace_recv,
            device_id=peer_of(offset),
            device_id_type=MESH,
        )

    def spread_records(offset, carry):
        trace_copy(offset).start()
        return carry

    lax.fori_loop(1, peers, spread_records, 0)
    for load in loads[4:]:
        load.wait()
    place(0, 0, source_prev)
    place(1, 0, receiver_prev)
    speed[:, :, full * LANES :] = jnp.zeros(
        (block_x, block_y, width - full * LANES), jnp.float32
    )
    speed[:, :, 0:depth] = speed_squared[...]
    for x in range(block_x):
        flat = ((me_x * block_x + x) * grid_y + me_y * block_y + row) * depth + lane
        hit = (flat == source_cell[0]) & (lane < depth)
        core[x] = jnp.where(hit, speed[x], 0.0)

    def source_extra(step):
        return lambda x, latest: latest + wavelet[step] * core[x]

    def receiver_extra(step):
        back = total_steps - 1 - step

        def add(x, latest):
            return jnp.concatenate(
                [latest[:, :LANES] + inject[back, x], latest[:, LANES:]], axis=1
            )

        return add

    def collect_planes():
        everything = pltpu.make_async_remote_copy(
            src_ref=gathered.at[pl.ds(0, peers - 1)],
            dst_ref=gathered.at[pl.ds(0, peers - 1)],
            send_sem=trace_send,
            recv_sem=trace_recv,
            device_id=there[0],
            device_id_type=MESH,
        )
        everything.wait()
        gathered[peers - 1] = records[...]
        cells = block_x * block_y
        number = lax.broadcasted_iota(jnp.int32, (cells, own), 0)
        number = (me_x * block_x + number // block_y) * grid_y + me_y * block_y + number % block_y
        number = number.astype(jnp.float32)

        def one(slot):
            block = gathered[slot]
            chosen = (block[total_steps : total_steps + 1, :] == number).astype(jnp.float32)
            return lax.dot_general(
                chosen,
                block,
                (((1,), (1,)), ((), ())),
                precision=lax.Precision.HIGHEST,
                preferred_element_type=jnp.float32,
            )

        group = 16 if peers % 16 == 0 else 1

        def several(index, total):
            for j in range(group):
                total = total + one(index * group + j)
            return total

        total = lax.fori_loop(
            0, peers // group, several, jnp.zeros((cells, records.shape[0]), jnp.float32)
        )
        planes[...] = jnp.zeros_like(planes)
        planes[:, 0 : records.shape[0]] = total
        for x in range(block_x):
            rows = planes[x * block_y : (x + 1) * block_y, :]
            for step in range(total_steps):
                turned = pltpu.roll(rows, (LANES - step) % LANES, axis=1) if step else rows
                inject[step, x] = jnp.where(tail_lane == 0, turned * speed[x, :, :LANES], 0.0)

    def both(step, carry):
        parity = lax.rem(step, 2)
        for field, extra in enumerate((source_extra, receiver_extra)):
            receive(field, step + 1, parity)
            if field == 1:
                pl.when(step == 0)(collect_planes)
            advance(field, step + 1, extra(step))

            @pl.when(step < total_steps - 1)
            def _():
                send(field, step + 2, 1 - parity)

        return carry

    lax.fori_loop(0, total_steps, both, 0)


def finish(
    total_steps,
    hist,
    plan,
    stored,
    image_before,
    out_source_prev,
    out_source_now,
    out_receiver_prev,
    out_receiver_now,
    out_snapshots,
    out_image,
):
    block_x, block_y, depth = image_before.shape
    inner = slice(HALF, HALF + block_x)
    out_source_prev[...] = hist[0, total_steps, inner, :, 0:depth]
    out_source_now[...] = hist[0, total_steps + 1, inner, :, 0:depth]
    out_receiver_prev[...] = hist[1, total_steps, inner, :, 0:depth]
    out_receiver_now[...] = hist[1, total_steps + 1, inner, :, 0:depth]
    total = image_before[...]
    for slot in range(plan.shape[0]):
        taken = hist[0, plan[slot] + 2, inner, :, 0:depth]
        out_snapshots[slot] = taken.astype(jnp.bfloat16)
        taken = hist[1, total_steps + 1 - plan[slot], inner, :, 0:depth]
        total = total + stored[slot].astype(jnp.float32) * taken
    out_image[...] = total


def body(*arrays):
    source_now, wavelet, traces, stored, plan = (arrays[i] for i in (1, 5, 7, 10, 9))
    block_x, block_y, depth = source_now.shape
    total_steps = wavelet.shape[0]
    own = traces.shape[1]
    peers = lax.axis_size("gx") * lax.axis_size("gy")
    width = -(-depth // LANES) * LANES
    record_rows = -(-(total_steps + 1) // 8) * 8
    tiles = HALF * depth // LANES
    vmem = pl.BlockSpec(memory_space=pltpu.VMEM)
    hbm = pl.BlockSpec(memory_space=pltpu.HBM)
    smem = pl.BlockSpec(memory_space=pltpu.SMEM)
    field = jax.ShapeDtypeStruct(source_now.shape, jnp.float32)
    f32 = jnp.float32
    shape = (2, total_steps + 2, block_x + 2 * HALF, block_y, width)
    hist = pl.pallas_call(
        functools.partial(kernel, total_steps),
        out_shape=pltpu.VMEM(shape, f32),
        in_specs=[hbm] * 6 + [smem] + [hbm] * 2,
        out_specs=vmem,
        scratch_shapes=[
            pltpu.VMEM((block_x, block_y, width), f32),
            pltpu.VMEM((block_x, block_y, width), f32),
            pltpu.VMEM((2, block_x, block_y, width), f32),
            pltpu.VMEM((2, 4, tiles, block_y, LANES), f32),
            pltpu.VMEM((2, 2, 4, tiles, block_y, LANES), f32),
            pltpu.VMEM((record_rows, own), f32),
            pltpu.VMEM((peers, record_rows, own), f32),
            pltpu.VMEM((block_x * block_y, LANES), f32),
            pltpu.VMEM((total_steps, block_x, block_y, LANES), f32),
            pltpu.SemaphoreType.DMA((2, 4)),
            pltpu.SemaphoreType.DMA((2, 2, 4)),
            pltpu.SemaphoreType.DMA,
            pltpu.SemaphoreType.DMA,
            pltpu.SemaphoreType.DMA((8,)),
            *[pltpu.VMEM(source_now.shape, f32)] * 5,
            pltpu.SMEM(wavelet.shape, f32),
            pltpu.VMEM(traces.shape, f32),
            pltpu.VMEM(arrays[8].shape, jnp.int32),
        ],
        compiler_params=pltpu.CompilerParams(
            collective_id=0, has_side_effects=True, vmem_limit_bytes=24 << 20
        ),
    )(
        *[
            array if i == 6 else pltpu.with_memory_space_constraint(array, pltpu.HBM)
            for i, array in enumerate(arrays[:9])
        ]
    )
    return pl.pallas_call(
        functools.partial(finish, total_steps),
        out_shape=(
            field,
            field,
            field,
            field,
            jax.ShapeDtypeStruct(stored.shape, jnp.bfloat16),
            field,
        ),
        in_specs=[vmem, smem, vmem, vmem],
        out_specs=[vmem] * 6,
        compiler_params=pltpu.CompilerParams(vmem_limit_bytes=24 << 20),
    )(hist, plan, stored, arrays[11])


def solution(mesh):
    block = P(("shot", "gx"), "gy", None)
    kept = P("shot", "gx", "gy", None)
    return jax.shard_map(
        body,
        mesh=mesh,
        in_specs=(
            block,
            block,
            block,
            block,
            block,
            P("shot"),
            P("shot"),
            P("shot", ("gx", "gy")),
            P("shot", ("gx", "gy")),
            P("shot"),
            kept,
            block,
        ),
        out_specs=(block, block, block, block, kept, block),
        check_vma=False,
    )
```

profile of v0, /device:TPU:0, one launch (start us, length us, event | category | flops | bytes accessed | tf_op | source)
XLA Modules:
  0.0 48.5 jit_solution(17575058901794209962)
XLA Ops:
  0.6 0.0 copy-start.1
  0.6 0.0 copy-start
  0.7 0.0 copy-start.2
  1.4 45.6 %shard_map.163.hist = f32[2,12,16,8,384]{4,3,2,1,0:T(8,128)S(1)} custom-call(f32[8,8,320]{2,1,0:T(8,128)} %source_prev_hbm.1, f32[8,8,320]{2,1,0:T(8,128)} %source_now_hbm.1, f32[8,8,320]{2,1,0:T(8,128)} %receiver_prev_hbm.1, f32[8,8,320]{2,1,0:T(8,128)} %receiver_now_hbm.1, f32[8,8,320]{2,1,0:T(8,128)} %speed_hbm.1, f32[10]{0:T(128)} %wavelet_hbm.1, ...), custom_call_target="tpu_custom_call" | custom-call | tf_op jit(solution)/shard_map/pallas_call | solution.py:361
  47.0 0.0 copy-done.1
  47.0 0.0 copy-done
  47.0 0.0 copy-done.2
  47.0 1.5 %shard_map.164 = (f32[8,8,320]{2,1,0:T(8,128)}, f32[8,8,320]{2,1,0:T(8,128)}, f32[8,8,320]{2,1,0:T(8,128)}, f32[8,8,320]{2,1,0:T(8,128)}, bf16[4,8,8,320]{3,2,1,0:T(8,128)(2,1)}, /*index=5*/f32[8,8,320]{2,1,0:T(8,128)}) custom-call(f32[2,12,16,8,384]{4,3,2,1,0:T(8,128)S(1)} %shard_map.163.hist, s32[4]{0:T(128)S(1)} %copy-done.2, ...), custom_call_target="tpu_custom_call" | custom-call | tf_op jit(solution)/shard_map/pallas_call | solution.py:395
Async XLA Ops:
  0.6 46.3 %copy-start.1 = (f32[8,8,320]{2,1,0:T(8,128)S(1)}, f32[8,8,320]{2,1,0:T(8,128)}, u32[]{:S(2)}) copy-start(f32[8,8,320]{2,1,0:T(8,128)} %image_before.1) | copy-start | bytes 245764
  0.6 46.3 %copy-start = (bf16[4,8,8,320]{3,2,1,0:T(8,128)(2,1)S(1)}, bf16[4,8,8,320]{3,2,1,0:T(8,128)(2,1)}, u32[]{:S(2)}) copy-start(bf16[4,8,8,320]{3,2,1,0:T(8,128)(2,1)} %stored.1) | copy-start | bytes 491524
  0.7 46.3 %copy-start.2 = (s32[4]{0:T(128)S(1)}, s32[4]{0:T(128)}, u32[]{:S(2)}) copy-start(s32[4]{0:T(128)} %plan.1) | copy-start | bytes 52
where the time goes:
time: 48.6 us; the launch traced here: 48.5 us
  Pallas kernels  47.1 us (97%)
  between operations  1.38 us (3%)
    pallas_call x1, Pallas kernels, body(): pl.pallas_call(functools.partial(kernel, total_steps), out_shape=pltpu.VM...  45.6 us
    pallas_call x1, Pallas kernels, body(): pl.pallas_call(functools.partial(finish, total_steps), out_shape=(field,...  1.47 us

commit v1 on v0

v1 whole, which is shorter than its diff:
```python
import functools
import jax
import jax.numpy as jnp
from jax import lax
from jax.experimental import pallas as pl
from jax.experimental.pallas import tpu as pltpu
from jax.sharding import PartitionSpec as P

STENCIL_COEFFS = (-205.0 / 72.0, 8.0 / 5.0, -1.0 / 5.0, 8.0 / 315.0, -1.0 / 560.0)
LANES = 128
HALF = 4
LOW_X, HIGH_X, LOW_Y, HIGH_Y = range(4)
OPPOSITE = (HIGH_X, LOW_X, HIGH_Y, LOW_Y)
MESH = pl.DeviceIdType.MESH


def kernel(
    total_steps,
    source_prev_hbm,
    source_now_hbm,
    receiver_prev_hbm,
    receiver_now_hbm,
    speed_hbm,
    wavelet_hbm,
    source_cell,
    traces_hbm,
    receiver_cells_hbm,
    hist,
    speed,
    core,
    packed,
    landed,
    records,
    gathered,
    planes,
    inject,
    send_sem,
    recv_sem,
    trace_send,
    trace_recv,
    load_sem,
    source_prev,
    source_now,
    receiver_prev,
    receiver_now,
    speed_squared,
    wavelet,
    traces,
    receiver_cells,
):
    loads = [
        pltpu.make_async_copy(start, end, load_sem.at[i])
        for i, (start, end) in enumerate(
            (
                (source_now_hbm, source_now),
                (receiver_now_hbm, receiver_now),
                (traces_hbm, traces),
                (receiver_cells_hbm, receiver_cells),
                (source_prev_hbm, source_prev),
                (receiver_prev_hbm, receiver_prev),
                (speed_hbm, speed_squared),
                (wavelet_hbm, wavelet),
            )
        )
    ]
    for load in loads:
        load.start()
    block_x, block_y, depth = source_now.shape
    count_x, count_y = lax.axis_size("gx"), lax.axis_size("gy")
    me_x, me_y = lax.axis_index("gx"), lax.axis_index("gy")
    grid_y = block_y * count_y
    peers = count_x * count_y
    me = me_x * count_y + me_y
    tiles = hist.shape[2]
    own = traces.shape[1]
    exists = (me_x > 0, me_x < count_x - 1, me_y > 0, me_y < count_y - 1)
    there = ({"gx": me_x - 1}, {"gx": me_x + 1}, {"gy": me_y - 1}, {"gy": me_y + 1})

    def peer_of(offset):
        other = lax.rem(me + offset, peers)
        return {"gx": other // count_y, "gy": lax.rem(other, count_y)}

    barrier = pltpu.get_barrier_semaphore()

    def greet(offset, carry):
        pl.semaphore_signal(barrier, inc=1, device_id=peer_of(offset), device_id_type=MESH)
        return carry

    lax.fori_loop(1, peers, greet, 0)

    for side in range(4):

        @pl.when(jnp.logical_not(exists[side]))
        def _():
            for field in range(2):
                for parity in range(2):
                    landed[field, parity, side] = jnp.zeros(landed.shape[3:], jnp.float32)

    row = lax.broadcasted_iota(jnp.int32, (block_y, LANES), 0)
    lane = lax.broadcasted_iota(jnp.int32, (block_y, LANES), 1)
    first_half = row < HALF
    spots = lax.rem(row, HALF)

    def only(mask, value):
        return jnp.where(mask, jnp.float32(value), jnp.float32(0.0))

    def turn(tile, shift):
        return pltpu.roll(tile, shift, axis=0) if shift else tile

    inner_y = [None] + [
        only(row >= s, STENCIL_COEFFS[s] if s <= HALF else 0.0)
        + only(row < s, STENCIL_COEFFS[block_y - s] if block_y - s <= HALF else 0.0)
        for s in range(1, block_y)
    ]
    upward = [only(spots < HALF - d, STENCIL_COEFFS[HALF - d]) for d in range(HALF)]
    downward = [only(spots >= d, STENCIL_COEFFS[HALF - d]) for d in range(HALF)]

    def cut(tile_index, array, x):
        low = tile_index * LANES
        size = min(LANES, depth - low)
        return array[x, :, low : low + size], size

    def place(target, array):
        for c in range(tiles):
            for x in range(block_x):
                part, size = cut(c, array, x)
                if size < LANES:
                    target[c, x] = jnp.zeros((block_y, LANES), jnp.float32)
                    target[c, x, :, 0:size] = part
                else:
                    target[c, x] = part

    def halo_copy(field, index, parity, side, into):
        if side == LOW_X:
            face = hist.at[field, index, :, 0:HALF]
        elif side == HIGH_X:
            face = hist.at[field, index, :, block_x - HALF : block_x]
        else:
            face = packed.at[field, side - LOW_Y]
        return pltpu.make_async_remote_copy(
            src_ref=face,
            dst_ref=landed.at[field, parity, into],
            send_sem=send_sem.at[field, side],
            recv_sem=recv_sem.at[field, parity, into],
            device_id=there[side],
            device_id_type=MESH,
        )

    def send(field, index, parity, side):
        @pl.when(exists[side])
        def _():
            halo_copy(field, index, parity, side, OPPOSITE[side]).start()

    def receive(field, index, parity, side):
        @pl.when(exists[side])
        def _():
            halo_copy(field, index, parity, side, side).wait()

    def pack_y(field, index):
        for c in range(tiles):
            for i in range(HALF):
                near, far = hist[field, index, c, i], hist[field, index, c, i + HALF]
                packed[field, 0, c, i] = jnp.where(first_half, near, turn(far, HALF))
                packed[field, 1, c, i] = jnp.where(first_half, turn(near, HALF), far)

    def add_y(field, index, parity):
        for c in range(tiles):
            for i in range(HALF):
                low, high = landed[field, parity, LOW_Y, c, i], landed[field, parity, HIGH_Y, c, i]
                below = upward[0] * low
                above = downward[0] * high
                for d in range(1, HALF):
                    below += upward[d] * turn(low, block_y - d)
                    above += downward[d] * turn(high, d)
                near = jnp.where(first_half, below, turn(above, HALF))
                far = jnp.where(first_half, turn(below, HALF), above)
                hist[field, index, c, i] += speed[c, i] * near
                hist[field, index, c, i + HALF] += speed[c, i + HALF] * far

    def add_x(field, index, parity, side):
        for c in range(tiles):
            faces = [landed[field, parity, side, c, j] for j in range(HALF)]
            for i in range(HALF):
                total = None
                for j in range(HALF):
                    distance = i + HALF - j if side == LOW_X else HALF + j - i
                    if distance <= HALF:
                        term = STENCIL_COEFFS[distance] * faces[j]
                        total = term if total is None else total + term
                x = i if side == LOW_X else block_x - HALF + i
                hist[field, index, c, x] += speed[c, x] * total

    def local(field, index, extra):
        for x in range(block_x):
            centers = [hist[field, index, c, x] for c in range(tiles)]
            spread = []
            for c in range(tiles):
                total = 3.0 * STENCIL_COEFFS[0] * centers[c]
                for s in range(1, block_y):
                    total += inner_y[s] * turn(centers[c], s)
                spread.append(total)
            for k in range(1, HALF + 1):
                forward = [pltpu.roll(center, k, axis=1) for center in centers]
                back = [pltpu.roll(center, LANES - k, axis=1) for center in centers]
                for c in range(tiles):
                    around = jnp.where(lane < k, forward[c - 1] if c else 0.0, forward[c])
                    around += jnp.where(
                        lane < LANES - k, back[c], back[c + 1] if c + 1 < tiles else 0.0
                    )
                    if x >= k:
                        around += hist[field, index, c, x - k]
                    if x + k < block_x:
                        around += hist[field, index, c, x + k]
                    spread[c] += STENCIL_COEFFS[k] * around
            for c in range(tiles):
                latest = 2.0 * centers[c] - hist[field, index - 1, c, x]
                hist[field, index + 1, c, x] = extra(c, x, latest + speed[c, x] * spread[c])

    for load in loads[:4]:
        load.wait()
    place(hist.at[0, 1], source_now)
    place(hist.at[1, 1], receiver_now)
    pack_y(0, 1)
    pack_y(1, 1)
    records[...] = jnp.zeros_like(records)
    records[0:total_steps, 0:own] = traces[...]
    records[total_steps : total_steps + 1, 0:own] = receiver_cells[...].astype(jnp.float32)
    pl.semaphore_wait(barrier, peers - 1)

    def trace_copy(offset):
        return pltpu.make_async_remote_copy(
            src_ref=records,
            dst_ref=gathered.at[offset - 1],
            send_sem=trace_send,
            recv_sem=trace_recv,
            device_id=peer_of(offset),
            device_id_type=MESH,
        )

    def spread_records(offset, carry):
        trace_copy(offset).start()
        return carry

    lax.fori_loop(1, peers, spread_records, 0)
    for field in range(2):
        for side in range(4):
            send(field, 1, 0, side)
    for load in loads[4:]:
        load.wait()
    place(hist.at[0, 0], source_prev)
    place(hist.at[1, 0], receiver_prev)
    place(speed, speed_squared)
    origin = jnp.broadcast_to(source_cell[...].reshape(1, 1), (block_y, LANES))
    for c in range(tiles):
        for x in range(block_x):
            flat = ((me_x * block_x + x) * grid_y + me_y * block_y + row) * depth + c * LANES + lane
            hit = flat == origin
            if (c + 1) * LANES > depth:
                hit &= lane < depth - c * LANES
            core[c, x] = jnp.where(hit, speed[c, x], 0.0)

    def source_extra(step):
        return lambda c, x, latest: latest + wavelet[step] * core[c, x]

    def receiver_extra(step):
        back = total_steps - 1 - step
        return lambda c, x, latest: latest if c else latest + inject[back, x]

    local(0, 1, source_extra(0))
    local(1, 1, lambda c, x, latest: latest)

    def injected(step, x):
        rows = planes[x * block_y : (x + 1) * block_y, :]
        turned = pltpu.roll(rows, LANES - step, axis=1) if step else rows
        return jnp.where(lane == 0, turned * speed[0, x], 0.0)

    def collect_planes():
        everything = pltpu.make_async_remote_copy(
            src_ref=gathered.at[pl.ds(0, peers - 1)],
            dst_ref=gathered.at[pl.ds(0, peers - 1)],
            send_sem=trace_send,
            recv_sem=trace_recv,
            device_id=there[0],
            device_id_type=MESH,
        )
        everything.wait()
        gathered[peers - 1] = records[...]
        cells = block_x * block_y
        number = lax.broadcasted_iota(jnp.int32, (cells, LANES), 0)
        number = (me_x * block_x + number // block_y) * grid_y + me_y * block_y + number % block_y
        number = number.astype(jnp.float32)
        share = LANES // own
        count = records.shape[0]

        def one(first):
            block = gathered[first]
            for j in range(1, share):
                block = block + pltpu.roll(gathered[first + j], j * own, axis=1)
            cell = block[total_steps : total_steps + 1, :]
            chosen = jnp.where(cell == number, jnp.float32(1.0), jnp.float32(0.0))
            high = block.astype(jnp.bfloat16)
            rest = block - high.astype(jnp.float32)
            middle = rest.astype(jnp.bfloat16)
            low = (rest - middle.astype(jnp.float32)).astype(jnp.bfloat16)
            return chosen.astype(jnp.bfloat16), jnp.concatenate([high, middle, low], axis=0)

        group = 16 if peers % 16 == 0 else share

        def several(index, total):
            parts = [one(index * group + j) for j in range(0, group, share)]
            return total + lax.dot_general(
                jnp.concatenate([part[0] for part in parts], axis=1),
                jnp.concatenate([part[1] for part in parts], axis=1),
                (((1,), (1,)), ((), ())),
                preferred_element_type=jnp.float32,
            )

        zero = jnp.zeros((cells, 3 * count), jnp.float32)
        total = several(0, zero) if peers == group else lax.fori_loop(0, peers // group, several, zero)
        planes[...] = jnp.zeros_like(planes)
        planes[:, 0 : 3 * count] = total
        whole = planes[...]
        planes[...] = (
            whole
            + pltpu.roll(whole, LANES - count, axis=1)
            + pltpu.roll(whole, LANES - 2 * count, axis=1)
        )

    def halos(field, step, parity, going):
        index = step + 2
        for side in (LOW_Y, HIGH_Y):
            receive(field, index, parity, side)
        add_y(field, index, parity)
        for side in (LOW_X, HIGH_X):
            receive(field, index, parity, side)
            add_x(field, index, parity, side)
            if going:
                send(field, index, 1 - parity, side)
        if going:
            pack_y(field, index)
            for side in (LOW_Y, HIGH_Y):
                send(field, index, 1 - parity, side)

    halos(0, 0, 0, total_steps > 1)
    if total_steps > 1:
        local(0, 2, source_extra(1))
    collect_planes()
    for x in range(block_x):
        hist[1, 2, 0, x] += injected(total_steps - 1, x)
    halos(1, 0, 0, total_steps > 1)
    for step in range(total_steps - 1):
        for x in range(block_x):
            inject[step, x] = injected(step, x)
    if total_steps > 1:
        local(1, 2, receiver_extra(1))

    def both(step, carry):
        parity = lax.rem(step, 2)
        for field, extra in enumerate((source_extra, receiver_extra)):
            halos(field, step, parity, True)
            local(field, step + 2, extra(step + 1))
        return carry

    lax.fori_loop(1, total_steps - 1, both, 0)
    if total_steps > 1:
        for field in range(2):
            halos(field, total_steps - 1, (total_steps - 1) % 2, False)


def finish(
    total_steps,
    hist,
    plan,
    stored,
    image_before,
    out_source_prev,
    out_source_now,
    out_receiver_prev,
    out_receiver_now,
    out_snapshots,
    out_image,
):
    block_x, block_y, depth = image_before.shape
    for c in range(hist.shape[2]):
        low = c * LANES
        size = min(LANES, depth - low)
        span = slice(low, low + size)
        out_source_prev[:, :, span] = hist[0, total_steps, c, :, :, 0:size]
        out_source_now[:, :, span] = hist[0, total_steps + 1, c, :, :, 0:size]
        out_receiver_prev[:, :, span] = hist[1, total_steps, c, :, :, 0:size]
        out_receiver_now[:, :, span] = hist[1, total_steps + 1, c, :, :, 0:size]
        total = image_before[:, :, span]
        for slot in range(plan.shape[0]):
            taken = hist[0, plan[slot] + 2, c, :, :, 0:size]
            out_snapshots[slot, :, :, span] = taken.astype(jnp.bfloat16)
            taken = hist[1, total_steps + 1 - plan[slot], c, :, :, 0:size]
            total = total + stored[slot, :, :, span].astype(jnp.float32) * taken
        out_image[:, :, span] = total


def body(*arrays):
    source_now, wavelet, traces, stored, plan = (arrays[i] for i in (1, 5, 7, 10, 9))
    block_x, block_y, depth = source_now.shape
    total_steps = wavelet.shape[0]
    peers = lax.axis_size("gx") * lax.axis_size("gy")
    tiles = -(-depth // LANES)
    record_rows = -(-(total_steps + 1) // 8) * 8
    vmem = pl.BlockSpec(memory_space=pltpu.VMEM)
    hbm = pl.BlockSpec(memory_space=pltpu.HBM)
    smem = pl.BlockSpec(memory_space=pltpu.SMEM)
    field = jax.ShapeDtypeStruct(source_now.shape, jnp.float32)
    f32 = jnp.float32
    shape = (2, total_steps + 2, tiles, block_x, block_y, LANES)
    face = (tiles, HALF, block_y, LANES)
    hist = pl.pallas_call(
        functools.partial(kernel, total_steps),
        out_shape=pltpu.VMEM(shape, f32),
        in_specs=[hbm] * 6 + [vmem] + [hbm] * 2,
        out_specs=vmem,
        scratch_shapes=[
            pltpu.VMEM(shape[2:], f32),
            pltpu.VMEM(shape[2:], f32),
            pltpu.VMEM((2, 2) + face, f32),
            pltpu.VMEM((2, 2, 4) + face, f32),
            pltpu.VMEM((record_rows, LANES), f32),
            pltpu.VMEM((peers, record_rows, LANES), f32),
            pltpu.VMEM((block_x * block_y, LANES), f32),
            pltpu.VMEM((total_steps, block_x, block_y, LANES), f32),
            pltpu.SemaphoreType.DMA((2, 4)),
            pltpu.SemaphoreType.DMA((2, 2, 4)),
            pltpu.SemaphoreType.DMA,
            pltpu.SemaphoreType.DMA,
            pltpu.SemaphoreType.DMA((8,)),
            *[pltpu.VMEM(source_now.shape, f32)] * 5,
            pltpu.SMEM(wavelet.shape, f32),
            pltpu.VMEM(traces.shape, f32),
            pltpu.VMEM(arrays[8].shape, jnp.int32),
        ],
        compiler_params=pltpu.CompilerParams(
            collective_id=0, has_side_effects=True, vmem_limit_bytes=24 << 20
        ),
    )(
        *[
            array if i == 6 else pltpu.with_memory_space_constraint(array, pltpu.HBM)
            for i, array in enumerate(arrays[:9])
        ]
    )
    return pl.pallas_call(
        functools.partial(finish, total_steps),
        out_shape=(
            field,
            field,
            field,
            field,
            jax.ShapeDtypeStruct(stored.shape, jnp.bfloat16),
            field,
        ),
        in_specs=[vmem, smem, vmem, vmem],
        out_specs=[vmem] * 6,
        compiler_params=pltpu.CompilerParams(vmem_limit_bytes=24 << 20),
    )(hist, plan, stored, arrays[11])


def solution(mesh):
    block = P(("shot", "gx"), "gy", None)
    kept = P("shot", "gx", "gy", None)
    return jax.shard_map(
        body,
        mesh=mesh,
        in_specs=(
            block,
            block,
            block,
            block,
            block,
            P("shot"),
            P("shot"),
            P("shot", ("gx", "gy")),
            P("shot", ("gx", "gy")),
            P("shot"),
            kept,
            block,
        ),
        out_specs=(block, block, block, block, kept, block),
        check_vma=False,
    )
```

time: 48.6 us -> 45.4 us (0.934)
  Pallas kernels: 47.1 us -> 43.9 us
    pallas_call x1, Pallas kernels: 45.6 us -> 42.4 us  [body(): pl.pallas_call(functools.partial(kernel, total_steps), out_shape=pltpu.VM...]
where the time goes in v1:
time: 45.4 us; the launch traced here: 45.3 us
  Pallas kernels  43.9 us (97%)
  between operations  1.38 us (3%)
    pallas_call x1, Pallas kernels, body(): pl.pallas_call(functools.partial(kernel, total_steps), out_shape=pltpu.VM...  42.4 us
    pallas_call x1, Pallas kernels, body(): pl.pallas_call(functools.partial(finish, total_steps), out_shape=(field,...  1.48 us

profile of v1, /device:TPU:0, one launch (start us, length us, event | category | flops | bytes accessed | tf_op | source)
XLA Modules:
  0.0 45.3 jit_solution(10941572782049887397)
XLA Ops:
  0.6 0.0 copy-start.1
  0.6 0.0 copy-start
  0.7 0.0 copy-start.2
  1.4 42.4 %shard_map.163.hist = f32[2,12,3,8,8,128]{5,4,3,2,1,0:T(8,128)S(1)} custom-call(f32[8,8,320]{2,1,0:T(8,128)} %source_prev_hbm.1, f32[8,8,320]{2,1,0:T(8,128)} %source_now_hbm.1, f32[8,8,320]{2,1,0:T(8,128)} %receiver_prev_hbm.1, f32[8,8,320]{2,1,0:T(8,128)} %receiver_now_hbm.1, f32[8,8,320]{2,1,0:T(8,128)} %speed_hbm.1, f32[10]{0:T(128)} %wavelet_hbm.1, ...), custom_call_target="tpu_custom_call" | custom-call | tf_op jit(solution)/shard_map/pallas_call | solution.py:415
  43.8 0.0 copy-done.1
  43.8 0.0 copy-done
  43.8 0.0 copy-done.2
  43.8 1.5 %shard_map.164 = (f32[8,8,320]{2,1,0:T(8,128)}, f32[8,8,320]{2,1,0:T(8,128)}, f32[8,8,320]{2,1,0:T(8,128)}, f32[8,8,320]{2,1,0:T(8,128)}, bf16[4,8,8,320]{3,2,1,0:T(8,128)(2,1)}, /*index=5*/f32[8,8,320]{2,1,0:T(8,128)}) custom-call(f32[2,12,3,8,8,128]{5,4,3,2,1,0:T(8,128)S(1)} %shard_map.163.hist, s32[4]{0:T(128)S(1)} %copy-done.2, ...), custom_call_target="tpu_custom_call" | custom-call | tf_op jit(solution)/shard_map/pallas_call | solution.py:448
Async XLA Ops:
  0.6 43.1 %copy-start.1 = (f32[8,8,320]{2,1,0:T(8,128)S(1)}, f32[8,8,320]{2,1,0:T(8,128)}, u32[]{:S(2)}) copy-start(f32[8,8,320]{2,1,0:T(8,128)} %image_before.1) | copy-start | bytes 245764
  0.6 43.1 %copy-start = (bf16[4,8,8,320]{3,2,1,0:T(8,128)(2,1)S(1)}, bf16[4,8,8,320]{3,2,1,0:T(8,128)(2,1)}, u32[]{:S(2)}) copy-start(bf16[4,8,8,320]{3,2,1,0:T(8,128)(2,1)} %stored.1) | copy-start | bytes 491524
  0.7 43.1 %copy-start.2 = (s32[4]{0:T(128)S(1)}, s32[4]{0:T(128)}, u32[]{:S(2)}) copy-start(s32[4]{0:T(128)} %plan.1) | copy-start | bytes 52

commit v2 on v1

--- a/solution.py
+++ b/solution.py
@@ -30,14 +30,17 @@
     core,
     packed,
     landed,
-    records,
+    line,
     gathered,
     planes,
     inject,
     send_sem,
     recv_sem,
+    line_send,
+    line_recv,
     trace_send,
     trace_recv,
+    known,
     load_sem,
     source_prev,
     source_now,
@@ -69,24 +72,30 @@
     count_x, count_y = lax.axis_size("gx"), lax.axis_size("gy")
     me_x, me_y = lax.axis_index("gx"), lax.axis_index("gy")
     grid_y = block_y * count_y
-    peers = count_x * count_y
-    me = me_x * count_y + me_y
     tiles = hist.shape[2]
     own = traces.shape[1]
     exists = (me_x > 0, me_x < count_x - 1, me_y > 0, me_y < count_y - 1)
     there = ({"gx": me_x - 1}, {"gx": me_x + 1}, {"gy": me_y - 1}, {"gy": me_y + 1})
 
-    def peer_of(offset):
-        other = lax.rem(me + offset, peers)
-        return {"gx": other // count_y, "gy": lax.rem(other, count_y)}
+    def on_line(offset):
+        return {"gy": lax.rem(me_y + offset, count_y)}
+
+    def across(offset):
+        return {"gx": lax.rem(me_x + offset, count_x)}
 
     barrier = pltpu.get_barrier_semaphore()
 
     def greet(offset, carry):
-        pl.semaphore_signal(barrier, inc=1, device_id=peer_of(offset), device_id_type=MESH)
+        pl.semaphore_signal(barrier, inc=1, device_id=on_line(offset), device_id_type=MESH)
         return carry
 
-    lax.fori_loop(1, peers, greet, 0)
+    for side in (LOW_X, HIGH_X):
+
+        @pl.when(exists[side])
+        def _():
+            pl.semaphore_signal(barrier, inc=1, device_id=there[side], device_id_type=MESH)
+
+    lax.fori_loop(1, count_y, greet, 0)
 
     for side in range(4):
 
@@ -130,65 +139,62 @@
                 else:
                     target[c, x] = part
 
-    def halo_copy(field, index, parity, side, into):
+    def halo_copy(field, index, parity, side, c, into):
         if side == LOW_X:
-            face = hist.at[field, index, :, 0:HALF]
+            face = hist.at[field, index, c, 0:HALF]
         elif side == HIGH_X:
-            face = hist.at[field, index, :, block_x - HALF : block_x]
+            face = hist.at[field, index, c, block_x - HALF : block_x]
         else:
-            face = packed.at[field, side - LOW_Y]
+            face = packed.at[field, side - LOW_Y, c]
         return pltpu.make_async_remote_copy(
             src_ref=face,
-            dst_ref=landed.at[field, parity, into],
-            send_sem=send_sem.at[field, side],
-            recv_sem=recv_sem.at[field, parity, into],
+            dst_ref=landed.at[field, parity, into, c],
+            send_sem=send_sem.at[field, side, c],
+            recv_sem=recv_sem.at[field, parity, into, c],
             device_id=there[side],
             device_id_type=MESH,
         )
 
-    def send(field, index, parity, side):
+    def send(field, index, parity, side, c):
         @pl.when(exists[side])
         def _():
-            halo_copy(field, index, parity, side, OPPOSITE[side]).start()
-
-    def receive(field, index, parity, side):
+            halo_copy(field, index, parity, side, c, OPPOSITE[side]).start()
+
+    def receive(field, index, parity, side, c):
         @pl.when(exists[side])
         def _():
-            halo_copy(field, index, parity, side, side).wait()
-
-    def pack_y(field, index):
-        for c in range(tiles):
-            for i in range(HALF):
-                near, far = hist[field, index, c, i], hist[field, index, c, i + HALF]
-                packed[field, 0, c, i] = jnp.where(first_half, near, turn(far, HALF))
-                packed[field, 1, c, i] = jnp.where(first_half, turn(near, HALF), far)
-
-    def add_y(field, index, parity):
-        for c in range(tiles):
-            for i in range(HALF):
-                low, high = landed[field, parity, LOW_Y, c, i], landed[field, parity, HIGH_Y, c, i]
-                below = upward[0] * low
-                above = downward[0] * high
-                for d in range(1, HALF):
-                    below += upward[d] * turn(low, block_y - d)
-                    above += downward[d] * turn(high, d)
-                near = jnp.where(first_half, below, turn(above, HALF))
-                far = jnp.where(first_half, turn(below, HALF), above)
-                hist[field, index, c, i] += speed[c, i] * near
-                hist[field, index, c, i + HALF] += speed[c, i + HALF] * far
-
-    def add_x(field, index, parity, side):
-        for c in range(tiles):
-            faces = [landed[field, parity, side, c, j] for j in range(HALF)]
-            for i in range(HALF):
-                total = None
-                for j in range(HALF):
-                    distance = i + HALF - j if side == LOW_X else HALF + j - i
-                    if distance <= HALF:
-                        term = STENCIL_COEFFS[distance] * faces[j]
-                        total = term if total is None else total + term
-                x = i if side == LOW_X else block_x - HALF + i
-                hist[field, index, c, x] += speed[c, x] * total
+            halo_copy(field, index, parity, side, c, side).wait()
+
+    def pack_y(field, index, c):
+        for i in range(HALF):
+            near, far = hist[field, index, c, i], hist[field, index, c, i + HALF]
+            packed[field, 0, c, i] = jnp.where(first_half, near, turn(far, HALF))
+            packed[field, 1, c, i] = jnp.where(first_half, turn(near, HALF), far)
+
+    def add_y(field, index, parity, c):
+        for i in range(HALF):
+            low, high = landed[field, parity, LOW_Y, c, i], landed[field, parity, HIGH_Y, c, i]
+            below = upward[0] * low
+            above = downward[0] * high
+            for d in range(1, HALF):
+                below += upward[d] * turn(low, block_y - d)
+                above += downward[d] * turn(high, d)
+            near = jnp.where(first_half, below, turn(above, HALF))
+            far = jnp.where(first_half, turn(below, HALF), above)
+            hist[field, index, c, i] += speed[c, i] * near
+            hist[field, index, c, i + HALF] += speed[c, i + HALF] * far
+
+    def add_x(field, index, parity, side, c):
+        faces = [landed[field, parity, side, c, j] for j in range(HALF)]
+        for i in range(HALF):
+            total = None
+            for j in range(HALF):
+                distance = i + HALF - j if side == LOW_X else HALF + j - i
+                if distance <= HALF:
+                    term = STENCIL_COEFFS[distance] * faces[j]
+                    total = term if total is None else total + term
+            x = i if side == LOW_X else block_x - HALF + i
+            hist[field, index, c, x] += speed[c, x] * total
 
     def local(field, index, extra):
         for x in range(block_x):
@@ -220,35 +226,68 @@
         load.wait()
     place(hist.at[0, 1], source_now)
     place(hist.at[1, 1], receiver_now)
-    pack_y(0, 1)
-    pack_y(1, 1)
-    records[...] = jnp.zeros_like(records)
-    records[0:total_steps, 0:own] = traces[...]
-    records[total_steps : total_steps + 1, 0:own] = receiver_cells[...].astype(jnp.float32)
-    pl.semaphore_wait(barrier, peers - 1)
-
-    def trace_copy(offset):
+    for field in range(2):
+        for c in range(tiles):
+            pack_y(field, 1, c)
+    rows = -(-total_steps // 2)
+    mine = line.at[me_y]
+    mine[...] = jnp.zeros((block_y, LANES), jnp.float32)
+    mine[0:rows, 0:own] = traces[0:rows, :]
+    mine[0 : total_steps - rows, own : 2 * own] = traces[rows:total_steps, :]
+    mine[rows : rows + 1, 0:own] = receiver_cells[...].astype(jnp.float32)
+    mine[rows : rows + 1, own : 2 * own] = receiver_cells[...].astype(jnp.float32)
+    beside = [exists[side].astype(jnp.int32) for side in (LOW_X, HIGH_X)]
+    pl.semaphore_wait(barrier, count_y - 1 + beside[0] + beside[1])
+
+    def line_copy(offset):
         return pltpu.make_async_remote_copy(
-            src_ref=records,
-            dst_ref=gathered.at[offset - 1],
-            send_sem=trace_send,
-            recv_sem=trace_recv,
-            device_id=peer_of(offset),
+            src_ref=line.at[me_y],
+            dst_ref=line.at[me_y],
+            send_sem=line_send,
+            recv_sem=line_recv,
+            device_id=on_line(offset),
             device_id_type=MESH,
         )
 
-    def spread_records(offset, carry):
-        trace_copy(offset).start()
+    def spread_line(offset, carry):
+        line_copy(offset).start()
         return carry
 
-    lax.fori_loop(1, peers, spread_records, 0)
-    for field in range(2):
-        for side in range(4):
-            send(field, 1, 0, side)
+    def tell(turn_number):
+        for side in (LOW_X, HIGH_X):
+
+            @pl.when(exists[side])
+            def _():
+                pl.semaphore_signal(
+                    known.at[turn_number, OPPOSITE[side]],
+                    inc=1,
+                    device_id=there[side],
+                    device_id_type=MESH,
+                )
+
+    def hear(turn_number):
+        for side in (LOW_X, HIGH_X):
+
+            @pl.when(exists[side])
+            def _():
+                pl.semaphore_wait(known.at[turn_number, side], 1)
+
+    def pass_on(turn_number, carry):
+        hear(turn_number - 1)
+        tell(turn_number)
+        return carry
+
+    rounds = count_x - 2
+    lax.fori_loop(1, count_y, spread_line, 0)
+    if rounds > 0:
+        tell(0)
+    for c in range(tiles):
+        for field in range(2):
+            for side in range(4):
+                send(field, 1, 0, side, c)
     for load in loads[4:]:
         load.wait()
     place(hist.at[0, 0], source_prev)
-    place(hist.at[1, 0], receiver_prev)
     place(speed, speed_squared)
     origin = jnp.broadcast_to(source_cell[...].reshape(1, 1), (block_y, LANES))
     for c in range(tiles):
@@ -266,48 +305,79 @@
         back = total_steps - 1 - step
         return lambda c, x, latest: latest if c else latest + inject[back, x]
 
+    if rounds > 1:
+        lax.fori_loop(1, rounds, pass_on, 0)
     local(0, 1, source_extra(0))
+    if rounds > 0:
+        hear(rounds - 1)
+
+    def trace_copy(offset):
+        return pltpu.make_async_remote_copy(
+            src_ref=line,
+            dst_ref=gathered.at[me_x],
+            send_sem=trace_send,
+            recv_sem=trace_recv,
+            device_id=across(offset),
+            device_id_type=MESH,
+        )
+
+    def spread_traces(offset, carry):
+        trace_copy(offset).start()
+        return carry
+
+    everyone = pltpu.make_async_remote_copy(
+        src_ref=line.at[pl.ds(0, count_y - 1)],
+        dst_ref=line.at[pl.ds(0, count_y - 1)],
+        send_sem=line_send,
+        recv_sem=line_recv,
+        device_id=on_line(1),
+        device_id_type=MESH,
+    )
+    everyone.wait()
+    lax.fori_loop(1, count_x, spread_traces, 0)
+    gathered[me_x] = line[...]
+    place(hist.at[1, 0], receiver_prev)
     local(1, 1, lambda c, x, latest: latest)
 
     def injected(step, x):
-        rows = planes[x * block_y : (x + 1) * block_y, :]
-        turned = pltpu.roll(rows, LANES - step, axis=1) if step else rows
+        values = planes[x * block_y : (x + 1) * block_y, :]
+        spot = step if step < rows else block_y + step - rows
+        turned = pltpu.roll(values, LANES - spot, axis=1) if spot else values
         return jnp.where(lane == 0, turned * speed[0, x], 0.0)
 
     def collect_planes():
         everything = pltpu.make_async_remote_copy(
-            src_ref=gathered.at[pl.ds(0, peers - 1)],
-            dst_ref=gathered.at[pl.ds(0, peers - 1)],
+            src_ref=gathered.at[pl.ds(0, count_x - 1)],
+            dst_ref=gathered.at[pl.ds(0, count_x - 1)],
             send_sem=trace_send,
             recv_sem=trace_recv,
-            device_id=there[0],
+            device_id=across(1),
             device_id_type=MESH,
         )
         everything.wait()
-        gathered[peers - 1] = records[...]
         cells = block_x * block_y
         number = lax.broadcasted_iota(jnp.int32, (cells, LANES), 0)
         number = (me_x * block_x + number // block_y) * grid_y + me_y * block_y + number % block_y
         number = number.astype(jnp.float32)
-        share = LANES // own
-        count = records.shape[0]
-
-        def one(first):
-            block = gathered[first]
-            for j in range(1, share):
-                block = block + pltpu.roll(gathered[first + j], j * own, axis=1)
-            cell = block[total_steps : total_steps + 1, :]
-            chosen = jnp.where(cell == number, jnp.float32(1.0), jnp.float32(0.0))
-            high = block.astype(jnp.bfloat16)
-            rest = block - high.astype(jnp.float32)
+
+        def one(x, y):
+            block = gathered[x, y]
+            chosen = jnp.where(block[rows : rows + 1, :] == number, jnp.float32(1.0), jnp.float32(0.0))
+            both = jnp.concatenate(
+                [jnp.where(lane < own, block, 0.0), jnp.where(lane < own, 0.0, block)], axis=0
+            )
+            high = both.astype(jnp.bfloat16)
+            rest = both - high.astype(jnp.float32)
             middle = rest.astype(jnp.bfloat16)
             low = (rest - middle.astype(jnp.float32)).astype(jnp.bfloat16)
             return chosen.astype(jnp.bfloat16), jnp.concatenate([high, middle, low], axis=0)
 
-        group = 16 if peers % 16 == 0 else share
+        count = 2 * block_y
+        near = min(count_y, 4)
 
         def several(index, total):
-            parts = [one(index * group + j) for j in range(0, group, share)]
+            x, y = index // (count_y // near), lax.rem(index, count_y // near) * near
+            parts = [one(x, y + j) for j in range(near)]
             return total + lax.dot_general(
                 jnp.concatenate([part[0] for part in parts], axis=1),
                 jnp.concatenate([part[1] for part in parts], axis=1),
@@ -315,8 +385,13 @@
                 preferred_element_type=jnp.float32,
             )
 
-        zero = jnp.zeros((cells, 3 * count), jnp.float32)
-        total = several(0, zero) if peers == group else lax.fori_loop(0, peers // group, several, zero)
+        total = jnp.zeros((cells, 3 * count), jnp.float32)
+        groups = count_x * count_y // near
+        if groups <= 4:
+            for index in range(groups):
+                total = several(index, total)
+        else:
+            total = lax.fori_loop(0, groups, several, total)
         planes[...] = jnp.zeros_like(planes)
         planes[:, 0 : 3 * count] = total
         whole = planes[...]
@@ -328,18 +403,20 @@
 
     def halos(field, step, parity, going):
         index = step + 2
-        for side in (LOW_Y, HIGH_Y):
-            receive(field, index, parity, side)
-        add_y(field, index, parity)
-        for side in (LOW_X, HIGH_X):
-            receive(field, index, parity, side)
-            add_x(field, index, parity, side)
+        for c in range(tiles):
+            for side in (LOW_Y, HIGH_Y):
+                receive(field, index, parity, side, c)
+            add_y(field, index, parity, c)
+            for side in (LOW_X, HIGH_X):
+                receive(field, index, parity, side, c)
+            for side in (LOW_X, HIGH_X):
+                add_x(field, index, parity, side, c)
             if going:
-                send(field, index, 1 - parity, side)
-        if going:
-            pack_y(field, index)
-            for side in (LOW_Y, HIGH_Y):
-                send(field, index, 1 - parity, side)
+                for side in (LOW_X, HIGH_X):
+                    send(field, index, 1 - parity, side, c)
+                pack_y(field, index, c)
+                for side in (LOW_Y, HIGH_Y):
+                    send(field, index, 1 - parity, side, c)
 
     halos(0, 0, 0, total_steps > 1)
     if total_steps > 1:
@@ -402,9 +479,8 @@
     source_now, wavelet, traces, stored, plan = (arrays[i] for i in (1, 5, 7, 10, 9))
     block_x, block_y, depth = source_now.shape
     total_steps = wavelet.shape[0]
-    peers = lax.axis_size("gx") * lax.axis_size("gy")
+    count_x, count_y = lax.axis_size("gx"), lax.axis_size("gy")
     tiles = -(-depth // LANES)
-    record_rows = -(-(total_steps + 1) // 8) * 8
     vmem = pl.BlockSpec(memory_space=pltpu.VMEM)
     hbm = pl.BlockSpec(memory_space=pltpu.HBM)
     smem = pl.BlockSpec(memory_space=pltpu.SMEM)
@@ -422,14 +498,17 @@
             pltpu.VMEM(shape[2:], f32),
             pltpu.VMEM((2, 2) + face, f32),
             pltpu.VMEM((2, 2, 4) + face, f32),
-            pltpu.VMEM((record_rows, LANES), f32),
-            pltpu.VMEM((peers, record_rows, LANES), f32),
+            pltpu.VMEM((count_y, block_y, LANES), f32),
+            pltpu.VMEM((count_x, count_y, block_y, LANES), f32),
             pltpu.VMEM((block_x * block_y, LANES), f32),
             pltpu.VMEM((total_steps, block_x, block_y, LANES), f32),
-            pltpu.SemaphoreType.DMA((2, 4)),
-            pltpu.SemaphoreType.DMA((2, 2, 4)),
+            pltpu.SemaphoreType.DMA((2, 4, tiles)),
+            pltpu.SemaphoreType.DMA((2, 2, 4, tiles)),
             pltpu.SemaphoreType.DMA,
             pltpu.SemaphoreType.DMA,
+            pltpu.SemaphoreType.DMA,
+            pltpu.SemaphoreType.DMA,
+            pltpu.SemaphoreType.REGULAR((max(count_x - 2, 1), 2)),
             pltpu.SemaphoreType.DMA((8,)),
             *[pltpu.VMEM(source_now.shape, f32)] * 5,
             pltpu.SMEM(wavelet.shape, f32),

time: 45.4 us -> 41.7 us (0.919)
  Pallas kernels: 43.9 us -> 40.1 us
    pallas_call x1, Pallas kernels: 42.4 us -> 38.7 us  [body(): pl.pallas_call(functools.partial(kernel, total_steps), out_shape=pltpu.VM...]
where the time goes in v2:
time: 41.7 us; the launch traced here: 41.5 us
  Pallas kernels  40.1 us (96%)
  between operations  1.38 us (3%)
    pallas_call x1, Pallas kernels, body(): pl.pallas_call(functools.partial(kernel, total_steps), out_shape=pltpu.VM...  38.7 us
    pallas_call x1, Pallas kernels, body(): pl.pallas_call(functools.partial(finish, total_steps), out_shape=(field,...  1.48 us

profile of v2, /device:TPU:0, one launch (start us, length us, event | category | flops | bytes accessed | tf_op | source)
XLA Modules:
  0.0 41.5 jit_solution(18081038500635821384)
XLA Ops:
  0.6 0.0 copy-start.1
  0.6 0.0 copy-start
  0.7 0.0 copy-start.2
  1.4 38.7 %shard_map.163.hist = f32[2,12,3,8,8,128]{5,4,3,2,1,0:T(8,128)S(1)} custom-call(f32[8,8,320]{2,1,0:T(8,128)} %source_prev_hbm.1, f32[8,8,320]{2,1,0:T(8,128)} %source_now_hbm.1, f32[8,8,320]{2,1,0:T(8,128)} %receiver_prev_hbm.1, f32[8,8,320]{2,1,0:T(8,128)} %receiver_now_hbm.1, f32[8,8,320]{2,1,0:T(8,128)} %speed_hbm.1, f32[10]{0:T(128)} %wavelet_hbm.1, ...), custom_call_target="tpu_custom_call" | custom-call | tf_op jit(solution)/shard_map/pallas_call | solution.py:491
  40.0 0.0 copy-done.1
  40.0 0.0 copy-done
  40.0 0.0 copy-done.2
  40.0 1.5 %shard_map.164 = (f32[8,8,320]{2,1,0:T(8,128)}, f32[8,8,320]{2,1,0:T(8,128)}, f32[8,8,320]{2,1,0:T(8,128)}, f32[8,8,320]{2,1,0:T(8,128)}, bf16[4,8,8,320]{3,2,1,0:T(8,128)(2,1)}, /*index=5*/f32[8,8,320]{2,1,0:T(8,128)}) custom-call(f32[2,12,3,8,8,128]{5,4,3,2,1,0:T(8,128)S(1)} %shard_map.163.hist, s32[4]{0:T(128)S(1)} %copy-done.2, ...), custom_call_target="tpu_custom_call" | custom-call | tf_op jit(solution)/shard_map/pallas_call | solution.py:527
Async XLA Ops:
  0.6 39.4 %copy-start.1 = (f32[8,8,320]{2,1,0:T(8,128)S(1)}, f32[8,8,320]{2,1,0:T(8,128)}, u32[]{:S(2)}) copy-start(f32[8,8,320]{2,1,0:T(8,128)} %image_before.1) | copy-start | bytes 245764
  0.6 39.4 %copy-start = (bf16[4,8,8,320]{3,2,1,0:T(8,128)(2,1)S(1)}, bf16[4,8,8,320]{3,2,1,0:T(8,128)(2,1)}, u32[]{:S(2)}) copy-start(bf16[4,8,8,320]{3,2,1,0:T(8,128)(2,1)} %stored.1) | copy-start | bytes 491524
  0.7 39.4 %copy-start.2 = (s32[4]{0:T(128)S(1)}, s32[4]{0:T(128)}, u32[]{:S(2)}) copy-start(s32[4]{0:T(128)} %plan.1) | copy-start | bytes 52

commit v3 on v2

--- a/solution.py
+++ b/solution.py
@@ -30,6 +30,8 @@
     core,
     packed,
     landed,
+    speed_packed,
+    speed_landed,
     line,
     gathered,
     planes,
@@ -41,6 +43,8 @@
     trace_send,
     trace_recv,
     known,
+    speed_send,
+    speed_recv,
     load_sem,
     source_prev,
     source_now,
@@ -104,6 +108,7 @@
             for field in range(2):
                 for parity in range(2):
                     landed[field, parity, side] = jnp.zeros(landed.shape[3:], jnp.float32)
+            speed_landed[side] = jnp.zeros(speed_landed.shape[1:], jnp.float32)
 
     row = lax.broadcasted_iota(jnp.int32, (block_y, LANES), 0)
     lane = lax.broadcasted_iota(jnp.int32, (block_y, LANES), 1)
@@ -160,10 +165,11 @@
         def _():
             halo_copy(field, index, parity, side, c, OPPOSITE[side]).start()
 
-    def receive(field, index, parity, side, c):
+    def receive(field, index, parity, side, c, left=False):
         @pl.when(exists[side])
         def _():
-            halo_copy(field, index, parity, side, c, side).wait()
+            copy = halo_copy(field, index, parity, side, c, side)
+            copy.wait_recv() if left else copy.wait()
 
     def pack_y(field, index, c):
         for i in range(HALF):
@@ -287,8 +293,35 @@
                 send(field, 1, 0, side, c)
     for load in loads[4:]:
         load.wait()
+    place(speed, speed_squared)
+
+    def speed_copy(side, into):
+        if side == LOW_X:
+            face = speed.at[0, 0:HALF]
+        elif side == HIGH_X:
+            face = speed.at[0, block_x - HALF : block_x]
+        else:
+            face = speed_packed.at[side - LOW_Y]
+        return pltpu.make_async_remote_copy(
+            src_ref=face,
+            dst_ref=speed_landed.at[into],
+            send_sem=speed_send.at[side],
+            recv_sem=speed_recv.at[into],
+            device_id=there[side],
+            device_id_type=MESH,
+        )
+
+    for i in range(HALF):
+        near, far = speed[0, i], speed[0, i + HALF]
+        speed_packed[0, i] = jnp.where(first_half, near, turn(far, HALF))
+        speed_packed[1, i] = jnp.where(first_half, turn(near, HALF), far)
+    for side in range(4):
+
+        @pl.when(exists[side])
+        def _():
+            speed_copy(side, OPPOSITE[side]).start()
+
     place(hist.at[0, 0], source_prev)
-    place(speed, speed_squared)
     origin = jnp.broadcast_to(source_cell[...].reshape(1, 1), (block_y, LANES))
     for c in range(tiles):
         for x in range(block_x):
@@ -339,11 +372,11 @@
     place(hist.at[1, 0], receiver_prev)
     local(1, 1, lambda c, x, latest: latest)
 
-    def injected(step, x):
+    def injected(step, x, factor):
         values = planes[x * block_y : (x + 1) * block_y, :]
         spot = step if step < rows else block_y + step - rows
         turned = pltpu.roll(values, LANES - spot, axis=1) if spot else values
-        return jnp.where(lane == 0, turned * speed[0, x], 0.0)
+        return jnp.where(lane == 0, turned * factor, 0.0)
 
     def collect_planes():
         everything = pltpu.make_async_remote_copy(
@@ -355,10 +388,18 @@
             device_id_type=MESH,
         )
         everything.wait()
-        cells = block_x * block_y
-        number = lax.broadcasted_iota(jnp.int32, (cells, LANES), 0)
-        number = (me_x * block_x + number // block_y) * grid_y + me_y * block_y + number % block_y
-        number = number.astype(jnp.float32)
+        cells = planes.shape[0]
+        origin_x, origin_y = me_x * block_x, me_y * block_y
+        sites = [(origin_x + x, origin_y + row) for x in range(block_x)]
+        sites += [(origin_x - HALF + i, origin_y + row) for i in range(HALF)]
+        sites += [(origin_x + block_x + i, origin_y + row) for i in range(HALF)]
+        for edge in (origin_y - HALF, origin_y + block_y):
+            sites += [
+                (origin_x + i + jnp.where(first_half, 0, HALF), edge + spots) for i in range(HALF)
+            ]
+        number = jnp.concatenate(
+            [(at_x * grid_y + at_y).astype(jnp.float32) for at_x, at_y in sites], axis=0
+        )
 
         def one(x, y):
             block = gathered[x, y]
@@ -401,14 +442,26 @@
             + pltpu.roll(whole, LANES - 2 * count, axis=1)
         )
 
-    def halos(field, step, parity, going):
+    def patch(parity, side):
+        @pl.when(exists[side])
+        def _():
+            speed_copy(side, side).wait()
+            for i in range(HALF):
+                late = injected(total_steps - 1, block_x + side * HALF + i, speed_landed[side, i])
+                landed[1, parity, side, 0, i] += late
+
+    def halos(field, step, parity, going, patched=False):
         index = step + 2
         for c in range(tiles):
             for side in (LOW_Y, HIGH_Y):
                 receive(field, index, parity, side, c)
+                if patched and c == 0:
+                    patch(parity, side)
             add_y(field, index, parity, c)
             for side in (LOW_X, HIGH_X):
-                receive(field, index, parity, side, c)
+                receive(field, index, parity, side, c, patched and c == 0)
+                if patched and c == 0:
+                    patch(parity, side)
             for side in (LOW_X, HIGH_X):
                 add_x(field, index, parity, side, c)
             if going:
@@ -418,18 +471,27 @@
                 for side in (LOW_Y, HIGH_Y):
                     send(field, index, 1 - parity, side, c)
 
-    halos(0, 0, 0, total_steps > 1)
-    if total_steps > 1:
-        local(0, 2, source_extra(1))
+    halos(0, 0, 0, True)
+    local(0, 2, source_extra(1))
+    halos(1, 0, 0, True)
     collect_planes()
+    for side in (LOW_X, HIGH_X):
+
+        @pl.when(exists[side])
+        def _():
+            halo_copy(1, 2, 1, side, 0, side).wait_send()
+
     for x in range(block_x):
-        hist[1, 2, 0, x] += injected(total_steps - 1, x)
-    halos(1, 0, 0, total_steps > 1)
-    for step in range(total_steps - 1):
+        hist[1, 2, 0, x] += injected(total_steps - 1, x, speed[0, x])
+        inject[total_steps - 2, x] = injected(total_steps - 2, x, speed[0, x])
+    local(1, 2, receiver_extra(1))
+    halos(0, 1, 1, True)
+    for step in range(total_steps - 2):
         for x in range(block_x):
-            inject[step, x] = injected(step, x)
-    if total_steps > 1:
-        local(1, 2, receiver_extra(1))
+            inject[step, x] = injected(step, x, speed[0, x])
+    local(0, 3, source_extra(2))
+    halos(1, 1, 1, True, True)
+    local(1, 3, receiver_extra(2))
 
     def both(step, carry):
         parity = lax.rem(step, 2)
@@ -438,10 +500,9 @@
             local(field, step + 2, extra(step + 1))
         return carry
 
-    lax.fori_loop(1, total_steps - 1, both, 0)
-    if total_steps > 1:
-        for field in range(2):
-            halos(field, total_steps - 1, (total_steps - 1) % 2, False)
+    lax.fori_loop(2, total_steps - 1, both, 0)
+    for field in range(2):
+        halos(field, total_steps - 1, (total_steps - 1) % 2, False)
 
 
 def finish(
@@ -498,9 +559,11 @@
             pltpu.VMEM(shape[2:], f32),
             pltpu.VMEM((2, 2) + face, f32),
             pltpu.VMEM((2, 2, 4) + face, f32),
+            pltpu.VMEM((2,) + face[1:], f32),
+            pltpu.VMEM((4,) + face[1:], f32),
             pltpu.VMEM((count_y, block_y, LANES), f32),
             pltpu.VMEM((count_x, count_y, block_y, LANES), f32),
-            pltpu.VMEM((block_x * block_y, LANES), f32),
+            pltpu.VMEM(((block_x + 4 * HALF) * block_y, LANES), f32),
             pltpu.VMEM((total_steps, block_x, block_y, LANES), f32),
             pltpu.SemaphoreType.DMA((2, 4, tiles)),
             pltpu.SemaphoreType.DMA((2, 2, 4, tiles)),
@@ -509,6 +572,8 @@
             pltpu.SemaphoreType.DMA,
             pltpu.SemaphoreType.DMA,
             pltpu.SemaphoreType.REGULAR((max(count_x - 2, 1), 2)),
+            pltpu.SemaphoreType.DMA((4,)),
+            pltpu.SemaphoreType.DMA((4,)),
             pltpu.SemaphoreType.DMA((8,)),
             *[pltpu.VMEM(source_now.shape, f32)] * 5,
             pltpu.SMEM(wavelet.shape, f32),

time: 41.7 us -> 40.2 us (0.964)
  Pallas kernels: 40.1 us -> 38.6 us
    pallas_call x1, Pallas kernels: 38.7 us -> 37.2 us  [body(): pl.pallas_call(functools.partial(kernel, total_steps), out_shape=pltpu.VM...]
where the time goes in v3:
time: 40.2 us; the launch traced here: 40 us
  Pallas kernels  38.6 us (96%)
  between operations  1.38 us (3%)
    pallas_call x1, Pallas kernels, body(): pl.pallas_call(functools.partial(kernel, total_steps), out_shape=pltpu.VM...  37.2 us
    pallas_call x1, Pallas kernels, body(): pl.pallas_call(functools.partial(finish, total_steps), out_shape=(field,...  1.48 us

profile of v3, /device:TPU:0, one launch (start us, length us, event | category | flops | bytes accessed | tf_op | source)
XLA Modules:
  0.0 40.0 jit_solution(12797101031783890947)
XLA Ops:
  0.6 0.0 copy-start.1
  0.6 0.0 copy-start
  0.7 0.0 copy-start.2
  1.4 37.2 %shard_map.163.hist = f32[2,12,3,8,8,128]{5,4,3,2,1,0:T(8,128)S(1)} custom-call(f32[8,8,320]{2,1,0:T(8,128)} %source_prev_hbm.1, f32[8,8,320]{2,1,0:T(8,128)} %source_now_hbm.1, f32[8,8,320]{2,1,0:T(8,128)} %receiver_prev_hbm.1, f32[8,8,320]{2,1,0:T(8,128)} %receiver_now_hbm.1, f32[8,8,320]{2,1,0:T(8,128)} %speed_hbm.1, f32[10]{0:T(128)} %wavelet_hbm.1, ...), custom_call_target="tpu_custom_call" | custom-call | tf_op jit(solution)/shard_map/pallas_call | solution.py:552
  38.5 0.0 copy-done.1
  38.5 0.0 copy-done
  38.6 0.0 copy-done.2
  38.6 1.5 %shard_map.164 = (f32[8,8,320]{2,1,0:T(8,128)}, f32[8,8,320]{2,1,0:T(8,128)}, f32[8,8,320]{2,1,0:T(8,128)}, f32[8,8,320]{2,1,0:T(8,128)}, bf16[4,8,8,320]{3,2,1,0:T(8,128)(2,1)}, /*index=5*/f32[8,8,320]{2,1,0:T(8,128)}) custom-call(f32[2,12,3,8,8,128]{5,4,3,2,1,0:T(8,128)S(1)} %shard_map.163.hist, s32[4]{0:T(128)S(1)} %copy-done.2, ...), custom_call_target="tpu_custom_call" | custom-call | tf_op jit(solution)/shard_map/pallas_call | solution.py:592
Async XLA Ops:
  0.6 37.9 %copy-start.1 = (f32[8,8,320]{2,1,0:T(8,128)S(1)}, f32[8,8,320]{2,1,0:T(8,128)}, u32[]{:S(2)}) copy-start(f32[8,8,320]{2,1,0:T(8,128)} %image_before.1) | copy-start | bytes 245764
  0.6 37.9 %copy-start = (bf16[4,8,8,320]{3,2,1,0:T(8,128)(2,1)S(1)}, bf16[4,8,8,320]{3,2,1,0:T(8,128)(2,1)}, u32[]{:S(2)}) copy-start(bf16[4,8,8,320]{3,2,1,0:T(8,128)(2,1)} %stored.1) | copy-start | bytes 491524
  0.7 37.9 %copy-start.2 = (s32[4]{0:T(128)S(1)}, s32[4]{0:T(128)}, u32[]{:S(2)}) copy-start(s32[4]{0:T(128)} %plan.1) | copy-start | bytes 52
